TPU v7x, 32 devices: a whole 2x2x4 slice. The times are simulated.
32 devices in a mesh: dp: 8 (over z, x), row: 4 (over y, core).
Axes of the slice: x: 2, y: 2, z: 4, core: 2. Of those that a mesh axis runs over, the one named last changes fastest.
Arguments:
- queries: bfloat16 [2048, 4096], P('dp', 'row'), may hold values from -100 to 100
- passages: bfloat16 [2048, 4096], P('dp', 'row'), may hold values from -10 to 10
- cached: bfloat16 [16384, 4096], P('dp', 'row'), may hold values from -6 to 6
- hard_shard: int32 [2048, 4], P('dp'), may hold values from 0 to 7, as said below
- hard_row: int32 [2048, 4], P('dp'), may hold values from 0 to 2047
- query_source: int32 [2048], P('dp'), may hold values from 0 to 7
- block_source: int32 [16], replicated, may hold values from 0 to 7
Outputs:
- mean_loss: float32 [], replicated
- query_grad: bfloat16 [2048, 4096], P('dp', 'row')
- passage_grad: bfloat16 [2048, 4096], P('dp', 'row')
Inputs may be any that keep to these rules, and one draw needn't show every extreme that they name: `hard_shard`: one cache shard, drawn with the seed, is named exactly 256 times among the 256 queries of every device; among one device's queries no shard is named more than 256 times, and the other shards share the rest as evenly as possible; a query's 4 hard negatives lie in 4 different shards.
All inputs are finite; a program needn't handle non-finite values.
Results may differ from a plain program's by a relative error of at most 0.0043.
Values may be sent and summed in bfloat16 or wider, within the bound.
A program may use at most 128 MiB of HBM per device.

v0:
```python
import math

import jax
import jax.numpy as jnp
from jax import lax
from jax.sharding import PartitionSpec as P

D = 4096
BLOCK = 128


NEG_FILL = -1e30


def fetch_hard(cached, hard_shard, hard_row, n_data):
    row_count, hard_count = hard_shard.shape
    width_dev = cached.shape[1]
    capacity = min(row_count, 3 * row_count * hard_count // n_data)
    owners = hard_shard.reshape(-1)
    wanted = hard_row.reshape(-1)
    one_hot = (owners[:, None] == jnp.arange(n_data, dtype=jnp.int32)[None, :]).astype(jnp.int32)
    before = jnp.cumsum(one_hot, axis=0) - one_hot
    slot_index = jnp.sum(before * one_hot, axis=1)
    target = owners * capacity + slot_index
    requests = (
        jnp.zeros((n_data * capacity,), jnp.int32).at[target].set(wanted).reshape(n_data, capacity)
    )
    asked_rows = lax.all_to_all(requests, "dp", split_axis=0, concat_axis=0, tiled=True)
    picked = jnp.take(cached, asked_rows.reshape(-1), axis=0)
    picked = picked.reshape(asked_rows.shape[0], asked_rows.shape[1], width_dev)
    replies = lax.all_to_all(picked, "dp", split_axis=0, concat_axis=0, tiled=True)
    reply_rows = replies.reshape(n_data * capacity, width_dev)
    return jnp.take(reply_rows, target, axis=0).reshape(row_count, hard_count, width_dev)


def softmax_rows(summed, summed_hard, sources, block_source, first_row, logit_scale):
    logits = logit_scale * summed
    hard_logits = logit_scale * summed_hard
    columns = jnp.arange(logits.shape[1], dtype=jnp.int32)
    targets = first_row + jnp.arange(logits.shape[0], dtype=jnp.int32)
    column_source = jnp.repeat(block_source, BLOCK)
    positive = columns[None, :] == targets[:, None]
    allowed = (sources[:, None] != column_source[None, :]) | positive
    masked = jnp.where(allowed, logits, NEG_FILL)
    maximum = jnp.maximum(jnp.max(masked, axis=1), jnp.max(hard_logits, axis=1))
    exponent = jnp.exp(masked - maximum[:, None])
    hard_expo = jnp.exp(hard_logits - maximum[:, None])
    totals = jnp.sum(exponent, axis=1) + jnp.sum(hard_expo, axis=1)
    pos_logit = jnp.sum(jnp.where(positive, logits, 0.0), axis=1)
    per_query = maximum + jnp.log(totals) - pos_logit
    weights = (exponent / totals[:, None] - positive.astype(jnp.float32)).astype(jnp.bfloat16)
    hard_weights = (hard_expo / totals[:, None]).astype(jnp.bfloat16)
    return (weights, hard_weights, jnp.sum(per_query))


def on_device(queries, passages, cached, hard_shard, hard_row, query_source, block_source):
    row_count = queries.shape[0]
    n_data = lax.axis_size("dp")
    logit_scale = 1.0 / math.sqrt(D)
    hard_rows = fetch_hard(cached, hard_shard, hard_row, n_data)
    gathered = lax.all_gather(passages, "dp", axis=0, tiled=True)
    partial_logits = lax.dot_general(
        queries, gathered, (((1,), (1,)), ((), ())), preferred_element_type=jnp.float32
    )
    partial_hard = jnp.einsum("qd,qhd->qh", queries, hard_rows, preferred_element_type=jnp.float32)
    first_row = lax.axis_index("dp") * row_count
    summed, summed_hard = lax.psum((partial_logits, partial_hard), "row")
    weights, hard_weights, local_loss = softmax_rows(
        summed, summed_hard, query_source, block_source, first_row, logit_scale
    )
    loss_sum = lax.psum(local_loss, "dp")
    mean_loss = loss_sum / (row_count * n_data)
    query_grad = jnp.dot(weights, gathered, preferred_element_type=jnp.float32)
    query_grad = query_grad + jnp.einsum(
        "qh,qhd->qd", hard_weights, hard_rows, preferred_element_type=jnp.float32
    )
    passage_grad = lax.psum_scatter(
        lax.dot_general(
            weights, queries, (((0,), (0,)), ((), ())), preferred_element_type=jnp.float32
        ),
        "dp",
        scatter_dimension=0,
        tiled=True,
    )
    return (mean_loss, query_grad.astype(jnp.bfloat16), passage_grad.astype(jnp.bfloat16))


def solution(mesh):
    in_specs = (
        P("dp", "row"),
        P("dp", "row"),
        P("dp", "row"),
        P("dp", None),
        P("dp", None),
        P("dp"),
        P(),
    )
    out_specs = (P(), P("dp", "row"), P("dp", "row"))
    return jax.shard_map(
        on_device, mesh=mesh, in_specs=in_specs, out_specs=out_specs, check_vma=False
    )
```

profile of v0, /device:TPU:0, one launch (start us, length us, event | category | flops | bytes accessed | tf_op | source)
XLA Modules:
  0.0 395.2 jit_solution(5826302292346192708)
XLA Ops:
  7.2 0.7 broadcast_multiply_fusion
  7.9 0.8 copy.23
  8.7 0.1 eq.42
  8.9 0.1 reshape.142
  9.0 0.1 copy.27
  9.1 0.1 mul.43
  9.3 2.3 reduce-window.6
  11.5 0.3 slice_reduce_fusion
  11.8 0.2 reduce-window.9
  12.0 0.1 add_bitcast_fusion
  12.1 0.8 copy.28
  12.9 0.1 reshape.168
  13.1 4.9 %scatter_custom_fusion = s32[2048]{0:T(1024)} fusion(s32[1024]{0:T(1024)S(1)} %bitcast.48, s32[1024]{0:T(1024)S(1)} %reshape.168, s32[]{:T(128)} %constant.31.clone.1), kind=kCustom, calls=%fused_computation.35 | custom fusion | bytes 8196 | tf_op jit(solution)/shard_map/scatter | solution.py:26
  17.9 7.3 %all-to-all-start = ((s32[8,1,256]{2,1,0:T(1,128)}), s32[8,1,256]{2,1,0:T(1,128)S(1)}, u32[]{:S(2)}, u32[]{:S(2)}) async-start(s32[8,1,256]{2,1,0:T(1,128)} %bitcast.4), calls=%async_computation | async-start | bytes 16384 | tf_op jit(solution)/shard_map/all_to_all | solution.py:28
  25.2 0.0 all-gather.2.cloned.1.call-start
  25.3 0.7 all-gather.2.cloned.1.call-update
  26.0 5.8 %all-to-all-done = s32[8,1,256]{2,1,0:T(1,128)S(1)} async-done(((s32[8,1,256]{2,1,0:T(1,128)}), s32[8,1,256]{2,1,0:T(1,128)S(1)}, u32[]{:S(2)}, u32[]{:S(2)}) %all-to-all-start) | async-done | bytes 8224 | tf_op jit(solution)/shard_map/all_to_all | solution.py:28
  31.8 13.7 %gather_fusion = bf16[2048,1024]{1,0:T(8,128)(2,1)} fusion(bf16[2048,1024]{1,0:T(8,128)(2,1)} %param.9, s32[2048]{0:T(1024)S(1)} %broadcast_clamp_fusion), kind=kCustom, calls=%fused_computation | custom fusion | bytes 8396800 | tf_op jit(solution)/shard_map/jit(_take)/gather | solution.py:29
  45.5 3.9 broadcast_select_fusion
  49.4 4.7 %all-to-all-start.1 = ((bf16[8,256,1024]{2,1,0:T(8,128)(2,1)}), bf16[8,256,1024]{2,1,0:T(8,128)(2,1)}, u32[]{:S(2)}, u32[]{:S(2)}) async-start(bf16[8,256,1024]{2,1,0:T(8,128)(2,1)} %broadcast_select_fusion), calls=%async_computation.1 | async-start | bytes 8388608 | tf_op jit(solution)/shard_map/all_to_all | solution.py:31
  54.1 0.0 all-reduce.2.cloned.1.call-start
  54.2 0.1 reduce_sum.50
  54.3 0.1 copy.25
  54.4 120.1 %all-gather.2.cloned.1.call-done = bf16[2048,1024]{1,0:T(8,128)(2,1)} async-done(((bf16[256,1024]{1,0:T(8,128)(2,1)}), bf16[2048,1024]{1,0:T(8,128)(2,1)}) %all-gather.2.cloned.1.call-update) | async-done | bytes 4194320 | tf_op jit(solution)/shard_map/all_gather | solution.py:61
  174.5 4.8 %fusion.21 = f32[256,2048]{1,0:T(8,128)} fusion(bf16[256,1024]{1,0:T(8,128)(2,1)S(1)} %copy-done, bf16[2048,1024]{1,0:T(8,128)(2,1)} %all-gather.2.cloned.1.call-done), kind=kOutput, calls=%fused_computation.51 | convolution fusion | flops 1073741824 | bytes 6815744 | tf_op jit(solution)/shard_map/dot_general | solution.py:62
  179.3 0.0 all-reduce.2.cloned.1.call-update
  179.3 0.0 reduce-scatter.2.cloned.1.call-start
  179.4 0.2 copy.26
  179.6 0.4 copy-done.4
  179.9 0.1 broadcast_bitcast_fusion
  180.0 2.5 all-to-all-done.1
  182.5 7.7 %gather_fusion.1 = bf16[1024,1024]{1,0:T(8,128)(2,1)S(1)} fusion(bf16[2048,1024]{1,0:T(8,128)(2,1)} %bitcast.8, s32[1024]{0:T(1024)S(1)} %broadcast_clamp_fusion.1), kind=kCustom, calls=%fused_computation.1 | custom fusion | bytes 4198400 | tf_op jit(solution)/shard_map/jit(_take)/gather | solution.py:33
  190.2 2.2 gather.15
  192.4 4.6 %fusion.4 = f32[256,1,4]{2,1,0:T(1,128)S(1)} fusion(bf16[256,4,1024]{2,1,0:T(4,128)(2,1)} %gather.15, pred[256,4]{1,0:T(8,128)(4,1)S(1)} %copy.26, bf16[256,1024,1]{1,0,2:T(8,128)(2,1)S(1)} %bitcast.43), kind=kOutput, calls=%fused_computation.13 | convolution fusion | flops 3145728 | bytes 2626560 | tf_op jit(solution)/shard_map/qd,qhd->qh/dot_general | solution.py:65
  197.0 0.1 copy.30
  197.1 6.4 %psum.22 = f32[256,4]{0,1:T(4,128)S(1)} all-reduce(f32[256,4]{0,1:T(4,128)S(1)} %bitcast.51), channel_id=1, replica_groups=mesh['dp'=8,'row'=4] {'row'}, use_global_device_ids=true, to_apply=%region_6.7 | all-reduce | flops 1024 | bytes 8192 | tf_op jit(solution)/shard_map/psum | solution.py:67
  203.5 24.6 %all-reduce.2.cloned.1.call-done = f32[256,2048]{1,0:T(8,128)} async-done(((f32[256,2048]{1,0:T(8,128)}), f32[256,2048]{1,0:T(8,128)}) %all-reduce.2.cloned.1.call-update) | async-done | bytes 2097168 | tf_op jit(solution)/shard_map/psum | solution.py:67
  228.1 2.3 fusion.19
  230.5 1.5 fusion.2
  232.0 0.6 subtract_reduce_fusion
  232.6 5.1 %fusion.20 = f32[2048,1024]{1,0:T(8,128)} fusion(bf16[256,1024]{1,0:T(8,128)(2,1)S(1)} %copy-done, f32[256]{0:T(256)S(1)} %get-tuple-element.6, f32[256]{0:T(256)S(1)} %max.7, s32[256]{0:T(256)S(1)} %iota_add_fusion, f32[256,2048]{1,0:T(8,128)S(1)} %copy-done.1, s32[2048]{0:T(1024)S(1)} %broadcast_bitcast_fusion, s32[256]{0:T(256)S(1)} %copy-done.3), kind=kOutput, calls=%fused_computation.50 | convolution fusion | flops 1078984704 | bytes 11022336 | tf_op jit(solution)/shard_map/dot_general | solution.py:78
  237.7 0.0 reduce-scatter.2.cloned.1.call-update
  237.8 22.8 %psum.23 = f32[]{:T(128)} all-reduce(f32[]{:T(128)} %get-tuple-element.5), channel_id=1, replica_groups=mesh['dp'=8,'row'=4] {'dp'}, use_global_device_ids=true, to_apply=%region_12.13 | all-reduce | flops 1 | bytes 8 | tf_op jit(solution)/shard_map/psum | solution.py:71
  260.5 0.2 copy.31
  261.4 3.1 fusion.3
  264.5 2.5 fusion.5
  267.0 118.4 %reduce-scatter.2.cloned.1.call-done = f32[256,1024]{1,0:T(8,128)} async-done(((f32[2048,1024]{1,0:T(8,128)}), f32[256,1024]{1,0:T(8,128)}) %reduce-scatter.2.cloned.1.call-update) | async-done | bytes 1048592 | tf_op jit(solution)/shard_map/reduce_scatter | solution.py:77
  385.5 2.1 convert_element_type.28
  (24 shorter events, 0.2 us)
Async XLA Ops:
  7.2 167.3 %copy-start = (bf16[256,1024]{1,0:T(8,128)(2,1)S(1)}, bf16[256,1024]{1,0:T(8,128)(2,1)}, u32[]{:S(2)}) copy-start(bf16[256,1024]{1,0:T(8,128)(2,1)} %param.7) | copy-start | bytes 1572868
  17.9 13.8 %all-to-all-start = ((s32[8,1,256]{2,1,0:T(1,128)}), s32[8,1,256]{2,1,0:T(1,128)S(1)}, u32[]{:S(2)}, u32[]{:S(2)}) async-start(s32[8,1,256]{2,1,0:T(1,128)} %bitcast.4), calls=%async_computation | async-start | bytes 16384 | tf_op jit(solution)/shard_map/all_to_all | solution.py:28
  25.2 149.3 %all-gather.2.cloned.1.call-start = ((), (), s32[]{:S(2)}) async-start(), calls=%async_computation.3 | async-start | bytes 4718592 | tf_op jit(solution)/shard_map/all_gather | solution.py:61
  49.4 5.0 %copy-start.2 = (s32[256,4]{0,1:T(4,128)S(1)}, s32[256,4]{0,1:T(4,128)}, u32[]{:S(2)}) copy-start(s32[256,4]{0,1:T(4,128)} %param.10) | copy-start | bytes 12292
  49.4 133.1 %all-to-all-start.1 = ((bf16[8,256,1024]{2,1,0:T(8,128)(2,1)}), bf16[8,256,1024]{2,1,0:T(8,128)(2,1)}, u32[]{:S(2)}, u32[]{:S(2)}) async-start(bf16[8,256,1024]{2,1,0:T(8,128)(2,1)} %broadcast_select_fusion), calls=%async_computation.1 | async-start | bytes 8388608 | tf_op jit(solution)/shard_map/all_to_all | solution.py:31
  54.1 174.0 %all-reduce.2.cloned.1.call-start = ((), (), s32[]{:S(2)}) async-start(), calls=%async_computation.4 | async-start | bytes 4194304 | tf_op jit(solution)/shard_map/psum | solution.py:67
  179.3 0.7 copy-start.4
  179.3 206.2 %reduce-scatter.2.cloned.1.call-start = ((), (), s32[]{:S(2)}) async-start(), calls=%async_computation.5 | async-start | bytes 9437184 | tf_op jit(solution)/shard_map/reduce_scatter | solution.py:77
  192.4 35.7 %copy-start.3 = (s32[256]{0:T(256)S(1)}, s32[256]{0:T(256)}, u32[]{:S(2)}) copy-start(s32[256]{0:T(256)} %param.12) | copy-start | bytes 3076
  228.1 2.4 copy-start.1
  261.4 3.1 copy-start.5
Sparse Core Ops, SparseCore 0:
  28.2 146.2 all-gather.1
  179.4 48.6 all-reduce.1
  237.9 147.5 reduce-scatter.1
where the time goes:
time: 396 us; the launch traced here: 395 us
  waiting for transfers between devices  272 us (69%)
  local copies, waits for them, and re-layouts  32.2 us (8%)
  blocking collectives  29.1 us (7%)
  matrix products  20.1 us (5%)
  between operations  15.7 us (4%)
  other arithmetic  13.8 us (3%)
  starting transfers between devices  12.1 us (3%)
    all_gather x1, waiting for transfers between devices, on_device(): gathered = lax.all_gather(passages, 'dp', axis=0, tiled=True)  120 us
    reduce_scatter x1, waiting for transfers between devices, on_device(): lax.psum_scatter(lax.dot_general(weights, queries, (((0,), (0,)), ((), ()...  118 us
    psum x1, waiting for transfers between devices, on_device(): summed, summed_hard = lax.psum((partial_logits, partial_hard), 'row')  24.6 us
    psum x1, blocking collectives, on_device(): loss_sum = lax.psum(local_loss, 'dp')  22.8 us
    gather x1, local copies, waits for them, and re-layouts, fetch_hard(): picked = jnp.take(cached, asked_rows.reshape(-1), axis=0)  13.7 us
    gather x2, local copies, waits for them, and re-layouts, fetch_hard(): jnp.take(reply_rows, target, axis=0)  9.96 us
  transfers between devices with their start and end apart: 5, of which 5 were waited for; matrix products, arithmetic and copies ran while one was open for 11% of the time, Pallas kernels for 0%

commit v1 on v0

--- a/solution.py
+++ b/solution.py
@@ -1,15 +1,18 @@
+import functools
 import math
 
 import jax
 import jax.numpy as jnp
 from jax import lax
+from jax.experimental import pallas as pl
+from jax.experimental.pallas import tpu as pltpu
 from jax.sharding import PartitionSpec as P
 
 D = 4096
 BLOCK = 128
-
-
+LANES = 128
 NEG_FILL = -1e30
+MESH = pl.DeviceIdType.MESH
 
 
 def fetch_hard(cached, hard_shard, hard_row, n_data):
@@ -26,11 +29,355 @@
         jnp.zeros((n_data * capacity,), jnp.int32).at[target].set(wanted).reshape(n_data, capacity)
     )
     asked_rows = lax.all_to_all(requests, "dp", split_axis=0, concat_axis=0, tiled=True)
-    picked = jnp.take(cached, asked_rows.reshape(-1), axis=0)
+    picked = jnp.take(cached, asked_rows.reshape(-1), axis=0, mode="clip")
     picked = picked.reshape(asked_rows.shape[0], asked_rows.shape[1], width_dev)
     replies = lax.all_to_all(picked, "dp", split_axis=0, concat_axis=0, tiled=True)
     reply_rows = replies.reshape(n_data * capacity, width_dev)
-    return jnp.take(reply_rows, target, axis=0).reshape(row_count, hard_count, width_dev)
+    hard_rows = [
+        jnp.take(reply_rows, target.reshape(row_count, hard_count)[:, h], axis=0, mode="clip")
+        for h in range(hard_count)
+    ]
+    return hard_rows
+
+
+def gather_kernel(n, n_row, q_ref, p_ref, pall, qall, lsum, lpart, lrecv,
+                  gsend, grecv, lsend, lrecv_sem, own_sem):
+    me = lax.axis_index("dp")
+    r = lax.axis_index("row")
+    lines = n // 2
+    a = me // 2
+    b = me % 2
+    rows = q_ref.shape[0]
+    part = rows // n_row
+    across = a * 2 + 1 - b
+
+    barrier = pltpu.get_barrier_semaphore()
+    pl.semaphore_signal(barrier, inc=1, device_id=(across, r), device_id_type=MESH)
+    for k in range(1, n_row):
+        pl.semaphore_signal(
+            barrier, inc=1, device_id=(me, lax.rem(r + k, n_row)), device_id_type=MESH
+        )
+
+    @pl.when(a < lines - 1)
+    def _():
+        pl.semaphore_signal(barrier, inc=1, device_id=(me + 2, r), device_id_type=MESH)
+
+    @pl.when(a > 0)
+    def _():
+        pl.semaphore_signal(barrier, inc=1, device_id=(me - 2, r), device_id_type=MESH)
+
+    neighbours = (a < lines - 1).astype(jnp.int32) + (a > 0).astype(jnp.int32)
+    pl.semaphore_wait(barrier, n_row + neighbours)
+
+    alls = (pall, qall)
+    own = (p_ref, q_ref)
+
+    def copy(t, kind, blk, first=False):
+        to = (across, me + 2, me - 2)[kind]
+        return pltpu.make_async_remote_copy(
+            src_ref=own[t] if first else alls[t].at[blk],
+            dst_ref=alls[t].at[blk],
+            send_sem=gsend.at[t, kind, blk],
+            recv_sem=grecv.at[t, blk],
+            device_id=(to, r),
+            device_id_type=MESH,
+        )
+
+    def arrived(t, blk):
+        copy(t, 0, blk).wait_recv()
+
+    def start_own(t):
+        @pl.when(a < lines - 1)
+        def _():
+            copy(t, 1, me, True).start()
+
+        @pl.when(a > 0)
+        def _():
+            copy(t, 2, me, True).start()
+
+        copy(t, 0, me, True).start()
+
+    def multiply(blk, block):
+        lpart[blk] = lax.dot_general(
+            q_ref[...], block, (((1,), (1,)), ((), ())), preferred_element_type=jnp.float32
+        )
+
+    def ship(blk):
+        for k in range(1, n_row):
+            to = lax.rem(r + k, n_row)
+            ship_copy(blk, to, k).start()
+
+    def ship_copy(blk, to, k):
+        return pltpu.make_async_remote_copy(
+            src_ref=lpart.at[blk, pl.ds(pl.multiple_of(to * part, part), part), :],
+            dst_ref=lrecv.at[k - 1, blk],
+            send_sem=lsend.at[k - 1, blk],
+            recv_sem=lrecv_sem.at[k - 1, blk],
+            device_id=(me, to),
+            device_id_type=MESH,
+        )
+
+    def relay(t, s):
+        lo = me - 2 * (s + 1)
+        hi = me + 2 * (s + 1)
+
+        @pl.when(lo >= 0)
+        def _():
+            arrived(t, lo)
+
+            @pl.when(a < lines - 1)
+            def _():
+                copy(t, 1, lo).start()
+
+            copy(t, 0, lo).start()
+
+        @pl.when(hi < n)
+        def _():
+            arrived(t, hi)
+
+            @pl.when(a > 0)
+            def _():
+                copy(t, 2, hi).start()
+
+            copy(t, 0, hi).start()
+
+    def logits_of(s):
+        lo = me - 2 * (s + 1)
+        hi = me + 2 * (s + 1)
+        flip = 1 - 2 * b
+
+        @pl.when(lo >= 0)
+        def _():
+            multiply(lo, pall[lo])
+
+        @pl.when(hi < n)
+        def _():
+            multiply(hi, pall[hi])
+
+        @pl.when(lo >= 0)
+        def _():
+            ship(lo)
+            arrived(0, lo + flip)
+            multiply(lo + flip, pall[lo + flip])
+
+        @pl.when(hi < n)
+        def _():
+            ship(hi)
+            arrived(0, hi + flip)
+            multiply(hi + flip, pall[hi + flip])
+
+        @pl.when(lo >= 0)
+        def _():
+            ship(lo + flip)
+
+        @pl.when(hi < n)
+        def _():
+            ship(hi + flip)
+
+    start_own(0)
+    own_p = pltpu.make_async_copy(p_ref, pall.at[me], own_sem.at[0])
+    own_q = pltpu.make_async_copy(q_ref, qall.at[me], own_sem.at[1])
+    own_p.start()
+    own_q.start()
+    multiply(me, p_ref[...])
+    for s in range(lines - 1):
+        relay(0, s)
+        if s == lines - 2:
+            start_own(1)
+        if s == 0:
+            ship(me)
+            arrived(0, across)
+            multiply(across, pall[across])
+            ship(across)
+        else:
+            logits_of(s - 1)
+    for s in range(lines - 1):
+        relay(1, s)
+        if s == 0:
+            logits_of(lines - 2)
+    arrived(1, across)
+    flip = 1 - 2 * b
+    for s in range(lines - 1):
+        lo = me - 2 * (s + 1)
+        hi = me + 2 * (s + 1)
+
+        @pl.when(lo >= 0)
+        def _():
+            arrived(1, lo + flip)
+
+        @pl.when(hi < n)
+        def _():
+            arrived(1, hi + flip)
+
+    base = pl.multiple_of(r * part, part)
+    columns = p_ref.shape[0]
+    for blk in range(n):
+        total = lpart[blk, pl.ds(base, part), :]
+        for k in range(1, n_row):
+            ship_copy(blk, lax.rem(r + k, n_row), k).wait_recv()
+            total = total + lrecv[k - 1, blk]
+        lsum[:, blk * columns:(blk + 1) * columns] = total
+
+    own_p.wait()
+    own_q.wait()
+    for blk in range(n):
+        for k in range(1, n_row):
+            ship_copy(blk, lax.rem(r + k, n_row), k).wait_send()
+    for t in range(2):
+        copy(t, 0, me, True).wait_send()
+
+        @pl.when(a < lines - 1)
+        def _():
+            copy(t, 1, me, True).wait_send()
+
+        @pl.when(a > 0)
+        def _():
+            copy(t, 2, me, True).wait_send()
+
+        for s in range(lines - 1):
+            lo = me - 2 * (s + 1)
+            hi = me + 2 * (s + 1)
+
+            @pl.when(lo >= 0)
+            def _():
+                copy(t, 0, lo).wait_send()
+
+                @pl.when(a < lines - 1)
+                def _():
+                    copy(t, 1, lo).wait_send()
+
+            @pl.when(hi < n)
+            def _():
+                copy(t, 0, hi).wait_send()
+
+                @pl.when(a > 0)
+                def _():
+                    copy(t, 2, hi).wait_send()
+
+
+def gather_and_logits(queries, passages, n, n_row):
+    rows, width = queries.shape
+    prows = passages.shape[0]
+    part = rows // n_row
+    vmem = pl.BlockSpec(memory_space=pltpu.VMEM)
+    return pl.pallas_call(
+        functools.partial(gather_kernel, n, n_row),
+        name="gather_logits",
+        out_shape=(
+            jax.ShapeDtypeStruct((n, prows, width), passages.dtype),
+            jax.ShapeDtypeStruct((n, rows, width), queries.dtype),
+            jax.ShapeDtypeStruct((part, n * prows), jnp.float32),
+        ),
+        in_specs=[vmem, vmem],
+        out_specs=(vmem, vmem, vmem),
+        scratch_shapes=[
+            pltpu.VMEM((n, rows, prows), jnp.float32),
+            pltpu.VMEM((n_row - 1, n, part, prows), jnp.float32),
+            pltpu.SemaphoreType.DMA((2, 3, n)),
+            pltpu.SemaphoreType.DMA((2, n)),
+            pltpu.SemaphoreType.DMA((n_row - 1, n)),
+            pltpu.SemaphoreType.DMA((n_row - 1, n)),
+            pltpu.SemaphoreType.DMA((2,)),
+        ],
+        compiler_params=pltpu.CompilerParams(
+            collective_id=0, has_side_effects=True, vmem_limit_bytes=56 * 2**20
+        ),
+    )(queries, passages)
+
+
+def weights_kernel(n, n_row, columns, w_ref, wrow, wcol, dsend, drecv, rsend, rrecv, csend, crecv,
+                   own_sem):
+    me = lax.axis_index("dp")
+    r = lax.axis_index("row")
+    barrier = pltpu.get_barrier_semaphore()
+    for j in range(1, n):
+        pl.semaphore_signal(
+            barrier, inc=1, device_id=(lax.rem(me + j, n), r), device_id_type=MESH
+        )
+    for k in range(1, n_row):
+        pl.semaphore_signal(
+            barrier, inc=1, device_id=(me, lax.rem(r + k, n_row)), device_id_type=MESH
+        )
+    pl.semaphore_wait(barrier, n + n_row - 2)
+
+    def across(j):
+        to = lax.rem(me + j, n)
+        return pltpu.make_async_remote_copy(
+            src_ref=w_ref.at[:, pl.ds(pl.multiple_of(to * columns, columns), columns)],
+            dst_ref=wcol.at[r, me],
+            send_sem=dsend.at[j - 1],
+            recv_sem=drecv.at[j - 1],
+            device_id=(to, r),
+            device_id_type=MESH,
+        )
+
+    def along(k):
+        return pltpu.make_async_remote_copy(
+            src_ref=w_ref,
+            dst_ref=wrow.at[r],
+            send_sem=rsend.at[k - 1],
+            recv_sem=rrecv.at[k - 1],
+            device_id=(me, lax.rem(r + k, n_row)),
+            device_id_type=MESH,
+        )
+
+    def spread(k):
+        return pltpu.make_async_remote_copy(
+            src_ref=wcol.at[r],
+            dst_ref=wcol.at[r],
+            send_sem=csend.at[k - 1],
+            recv_sem=crecv.at[k - 1],
+            device_id=(me, lax.rem(r + k, n_row)),
+            device_id_type=MESH,
+        )
+
+    for j in range(1, n):
+        across(j).start()
+    for k in range(1, n_row):
+        along(k).start()
+    own_row = pltpu.make_async_copy(w_ref, wrow.at[r], own_sem.at[0])
+    own_col = pltpu.make_async_copy(
+        w_ref.at[:, pl.ds(pl.multiple_of(me * columns, columns), columns)],
+        wcol.at[r, me],
+        own_sem.at[1],
+    )
+    own_row.start()
+    own_col.start()
+    own_col.wait()
+    for j in range(1, n):
+        across(j).wait_recv()
+    for k in range(1, n_row):
+        spread(k).start()
+    own_row.wait()
+    for k in range(1, n_row):
+        along(k).wait_recv()
+        spread(k).wait_recv()
+    for j in range(1, n):
+        across(j).wait_send()
+    for k in range(1, n_row):
+        along(k).wait_send()
+        spread(k).wait_send()
+
+
+def exchange_weights(weights_ext, n, n_row, columns):
+    part, wide = weights_ext.shape
+    vmem = pl.BlockSpec(memory_space=pltpu.VMEM)
+    dma = pltpu.SemaphoreType.DMA
+    return pl.pallas_call(
+        functools.partial(weights_kernel, n, n_row, columns),
+        name="exchange_weights",
+        out_shape=(
+            jax.ShapeDtypeStruct((n_row, part, wide), weights_ext.dtype),
+            jax.ShapeDtypeStruct((n_row, n, part, columns), weights_ext.dtype),
+        ),
+        in_specs=[vmem],
+        out_specs=(vmem, vmem),
+        scratch_shapes=[
+            dma((n - 1,)), dma((n - 1,)), dma((n_row - 1,)), dma((n_row - 1,)),
+            dma((n_row - 1,)), dma((n_row - 1,)), dma((2,)),
+        ],
+        compiler_params=pltpu.CompilerParams(collective_id=1, has_side_effects=True),
+    )(weights_ext)
 
 
 def softmax_rows(summed, summed_hard, sources, block_source, first_row, logit_scale):
@@ -54,33 +401,47 @@
 
 
 def on_device(queries, passages, cached, hard_shard, hard_row, query_source, block_source):
-    row_count = queries.shape[0]
+    row_count, width = queries.shape
+    columns = passages.shape[0]
     n_data = lax.axis_size("dp")
+    n_row = lax.axis_size("row")
+    part = row_count // n_row
     logit_scale = 1.0 / math.sqrt(D)
     hard_rows = fetch_hard(cached, hard_shard, hard_row, n_data)
-    gathered = lax.all_gather(passages, "dp", axis=0, tiled=True)
-    partial_logits = lax.dot_general(
-        queries, gathered, (((1,), (1,)), ((), ())), preferred_element_type=jnp.float32
-    )
-    partial_hard = jnp.einsum("qd,qhd->qh", queries, hard_rows, preferred_element_type=jnp.float32)
-    first_row = lax.axis_index("dp") * row_count
-    summed, summed_hard = lax.psum((partial_logits, partial_hard), "row")
+    hard_count = len(hard_rows)
+    pall, qall, summed = gather_and_logits(queries, passages, n_data, n_row)
+    q32 = queries.astype(jnp.float32)
+    partial_hard = jnp.stack(
+        [jnp.sum(q32 * rows.astype(jnp.float32), axis=1) for rows in hard_rows], axis=1
+    )
+    summed_hard = lax.psum(partial_hard, "row")
+    row_at = lax.axis_index("row") * part
+    first_row = lax.axis_index("dp") * row_count + row_at
+    my_hard = lax.dynamic_slice_in_dim(summed_hard, row_at, part, 0)
+    my_source = lax.dynamic_slice_in_dim(query_source, row_at, part, 0)
     weights, hard_weights, local_loss = softmax_rows(
-        summed, summed_hard, query_source, block_source, first_row, logit_scale
-    )
-    loss_sum = lax.psum(local_loss, "dp")
+        summed, my_hard, my_source, block_source, first_row, logit_scale
+    )
+    n_all = weights.shape[1]
+    ext = jnp.concatenate(
+        [weights, jnp.pad(hard_weights, ((0, 0), (0, LANES - hard_count)))], axis=1
+    )
+    wrow, wcol = exchange_weights(ext, n_data, n_row, columns)
+    loss_sum = lax.psum(local_loss, ("dp", "row"))
     mean_loss = loss_sum / (row_count * n_data)
-    query_grad = jnp.dot(weights, gathered, preferred_element_type=jnp.float32)
-    query_grad = query_grad + jnp.einsum(
-        "qh,qhd->qd", hard_weights, hard_rows, preferred_element_type=jnp.float32
-    )
-    passage_grad = lax.psum_scatter(
-        lax.dot_general(
-            weights, queries, (((0,), (0,)), ((), ())), preferred_element_type=jnp.float32
-        ),
-        "dp",
-        scatter_dimension=0,
-        tiled=True,
+    wrow = wrow.reshape(row_count, n_all + LANES)
+    query_grad = jnp.dot(
+        wrow[:, :n_all], pall.reshape(n_data * columns, width), preferred_element_type=jnp.float32
+    )
+    for h in range(hard_count):
+        query_grad = query_grad + wrow[:, n_all + h:n_all + h + 1].astype(
+            jnp.float32
+        ) * hard_rows[h].astype(jnp.float32)
+    passage_grad = lax.dot_general(
+        wcol.reshape(n_row, n_data, part, columns),
+        qall.reshape(n_data, n_row, part, width).transpose(1, 0, 2, 3),
+        (((0, 1, 2), (0, 1, 2)), ((), ())),
+        preferred_element_type=jnp.float32,
     )
     return (mean_loss, query_grad.astype(jnp.bfloat16), passage_grad.astype(jnp.bfloat16))
 

time: 396 us -> 346 us (0.87)
  waiting for transfers between devices: 272 us -> 0.01 us
  Pallas kernels: 0 us -> 219 us
  blocking collectives: 29.1 us -> 63.7 us
  matrix products: 20.1 us -> 7.06 us
  between operations: 15.7 us -> 2.81 us
  starting transfers between devices: 12.1 us -> 4.73 us
  local copies, waits for them, and re-layouts: 32.2 us -> 38.8 us
  other arithmetic: 13.8 us -> 8.38 us
    pallas_call x0 -> x2, Pallas kernels: none -> 219 us  [the longest x1 190 us: gather_and_logits(): pl.pallas_call(functools.partial(gather_kernel, n, n_row), name='gather_l...]
    all_gather x1 -> x0, waiting for transfers between devices: 120 us -> none  [on_device(): gathered = lax.all_gather(passages, 'dp', axis=0, tiled=True)]
    reduce_scatter x1 -> x0, waiting for transfers between devices: 118 us -> none  [on_device(): lax.psum_scatter(lax.dot_general(weights, queries, (((0,), (0,)), ((), ()...]
    psum x1 -> x0, waiting for transfers between devices: 24.6 us -> none  [on_device(): summed, summed_hard = lax.psum((partial_logits, partial_hard), 'row')]
    psum x2, blocking collectives: 29.1 us -> 50.1 us  [the longest x1 38.6 us: on_device(): loss_sum = lax.psum(local_loss, ('dp', 'row'))]
    all_to_all x0 -> x1, blocking collectives: none -> 13.6 us  [fetch_hard(): lax.all_to_all(requests, 'dp', split_axis=0, concat_axis=0, tiled=True)]
    dot_general x5 -> x2, matrix products: 20.1 us -> 7.06 us  [the longest x1 4.73 us: on_device(): lax.dot_general(wcol.reshape(n_row, n_data, part, columns), qall.reshape(...]
    all_to_all x1 -> x0, starting transfers between devices: 7.28 us -> none  [fetch_hard(): lax.all_to_all(requests, 'dp', split_axis=0, concat_axis=0, tiled=True)]
  transfers between devices with their start and end apart: 5 -> 1, of which waited for: 5 -> 0; matrix products, arithmetic and copies ran while one was open for 11% -> 1% of each run, Pallas kernels for 0% -> 55%
where the time goes in v1:
time: 346 us; the launch traced here: 344 us
  Pallas kernels  219 us (63%)
  blocking collectives  63.7 us (18%)
  local copies, waits for them, and re-layouts  38.8 us (11%)
  other arithmetic  8.38 us (2%)
  matrix products  7.06 us (2%)
  starting transfers between devices  4.73 us (1%)
    pallas_call x1, Pallas kernels, gather_and_logits(): pl.pallas_call(functools.partial(gather_kernel, n, n_row), name='gather_l...  190 us
    psum x1, blocking collectives, on_device(): loss_sum = lax.psum(local_loss, ('dp', 'row'))  38.6 us
    pallas_call x1, Pallas kernels, exchange_weights(): pl.pallas_call(functools.partial(weights_kernel, n, n_row, columns), name...  29 us
    gather x4, local copies, waits for them, and re-layouts, fetch_hard(): jnp.take(reply_rows, target.reshape(row_count, hard_count)[:, h], axis=0,...  17.3 us
    gather x1, local copies, waits for them, and re-layouts, fetch_hard(): picked = jnp.take(cached, asked_rows.reshape(-1), axis=0, mode='clip')  13.7 us
    all_to_all x1, blocking collectives, fetch_hard(): lax.all_to_all(requests, 'dp', split_axis=0, concat_axis=0, tiled=True)  13.6 us
    psum x1, blocking collectives, on_device(): summed_hard = lax.psum(partial_hard, 'row')  11.5 us
  transfers between devices with their start and end apart: 1, of which 0 were waited for; matrix products, arithmetic and copies ran while one was open for 1% of the time, Pallas kernels for 55%

profile of v1, /device:TPU:0, one launch (start us, length us, event | category | flops | bytes accessed | tf_op | source)
XLA Modules:
  0.0 344.0 jit_solution(8510323925023471877)
XLA Ops:
  0.6 0.0 copy-start
  0.6 0.8 copy.37
  1.5 0.1 eq.45
  1.6 0.1 eq.41
  1.7 2.3 reduce-window.6
  4.0 0.3 slice_reduce_fusion.4
  4.3 0.2 reduce-window.9
  4.4 0.1 add_bitcast_fusion
  4.6 0.1 reduce_sum.87
  4.7 0.1 mul.108
  4.8 0.8 copy.40
  5.7 0.1 reshape.153
  5.8 4.3 %scatter_custom_fusion = s32[2048]{0:T(1024)S(1)} fusion(s32[1024]{0:T(1024)S(1)} %bitcast.65, s32[1024]{0:T(1024)S(1)} %reshape.153, s32[]{:T(128)} %constant.15.clone.1), kind=kCustom, calls=%fused_computation.69 | custom fusion | bytes 8196 | tf_op jit(solution)/shard_map/scatter | solution.py:29
  10.1 13.6 %all_to_all.14 = s32[8,1,256]{2,1,0:T(1,128)S(1)} all-to-all(s32[8,1,256]{2,1,0:T(1,128)S(1)} %bitcast.58), channel_id=1, replica_groups=mesh['dp'=8,'row'=4] {'dp'}, dimensions={0} | all-to-all | bytes 16384 | tf_op jit(solution)/shard_map/all_to_all | solution.py:31
  23.7 13.7 %gather_fusion = bf16[2048,1024]{1,0:T(8,128)(2,1)} fusion(bf16[2048,1024]{1,0:T(8,128)(2,1)} %param.9, s32[2048]{0:T(1024)S(1)} %broadcast_clamp_fusion), kind=kCustom, calls=%fused_computation | custom fusion | bytes 8396800 | tf_op jit(solution)/shard_map/jit(_take)/gather | solution.py:32
  37.4 4.7 %all-to-all-start.1 = ((bf16[8,256,1024]{2,1,0:T(8,128)(2,1)}), bf16[8,256,1024]{2,1,0:T(8,128)(2,1)}, u32[]{:S(2)}, u32[]{:S(2)}) async-start(bf16[8,256,1024]{2,1,0:T(8,128)(2,1)} %bitcast.54), calls=%async_computation.1 | async-start | bytes 8388608 | tf_op jit(solution)/shard_map/all_to_all | solution.py:34
  42.2 0.0 copy-done.5
  42.2 0.1 dynamic_slice.6
  42.3 189.6 %gather_logits.1 = (bf16[8,256,1024]{2,1,0:T(8,128)(2,1)}, bf16[8,256,1024]{2,1,0:T(8,128)(2,1)}, f32[64,2048]{1,0:T(8,128)}) custom-call(bf16[256,1024]{1,0:T(8,128)(2,1)} %q_ref.1, bf16[256,1024]{1,0:T(8,128)(2,1)} %p_ref.1), custom_call_target="tpu_custom_call" | custom-call | tf_op jit(solution)/shard_map/gather_logits/pallas_call | solution.py:263
  231.9 0.3 slice_reduce_fusion.3
  232.3 0.0 copy-done
  232.3 0.1 broadcast_bitcast_fusion
  232.4 1.3 fusion.32
  233.7 0.0 all-to-all-done.1
  233.7 4.3 %gather_fusion.4 = bf16[256,1024]{1,0:T(8,128)(2,1)S(1)} fusion(bf16[2048,1024]{1,0:T(8,128)(2,1)} %bitcast.7, s32[1024]{0:T(1024)S(1)} %get-tuple-element.31), kind=kCustom, calls=%fused_computation.4 | custom fusion | bytes 1049600 | tf_op jit(solution)/shard_map/jit(_take)/gather | solution.py:37
  238.0 4.3 %gather_fusion.3 = bf16[256,1024]{1,0:T(8,128)(2,1)S(1)} fusion(bf16[2048,1024]{1,0:T(8,128)(2,1)} %bitcast.7, s32[1024]{0:T(1024)S(1)} %get-tuple-element.32), kind=kCustom, calls=%fused_computation.3 | custom fusion | bytes 1049600 | tf_op jit(solution)/shard_map/jit(_take)/gather | solution.py:37
  242.3 0.0 copy-start.2
  242.3 4.3 %gather_fusion.2 = bf16[256,1024]{1,0:T(8,128)(2,1)S(1)} fusion(bf16[2048,1024]{1,0:T(8,128)(2,1)} %bitcast.7, s32[1024]{0:T(1024)S(1)} %get-tuple-element.33), kind=kCustom, calls=%fused_computation.2 | custom fusion | bytes 1049600 | tf_op jit(solution)/shard_map/jit(_take)/gather | solution.py:37
  246.6 4.3 %gather_fusion.1 = bf16[256,1024]{1,0:T(8,128)(2,1)S(1)} fusion(bf16[2048,1024]{1,0:T(8,128)(2,1)} %bitcast.7, s32[1024]{0:T(1024)S(1)} %get-tuple-element.34), kind=kCustom, calls=%fused_computation.1 | custom fusion | bytes 1049600 | tf_op jit(solution)/shard_map/jit(_take)/gather | solution.py:37
  251.0 0.6 fusion.13
  251.6 0.1 copy.41
  251.8 11.5 %psum.14 = f32[256,4]{1,0:T(8,128)S(1)} all-reduce(f32[256,4]{1,0:T(8,128)S(1)} %copy.41), channel_id=1, replica_groups=mesh['dp'=8,'row'=4] {'row'}, use_global_device_ids=true, to_apply=%region_9.10 | all-reduce | flops 1024 | bytes 8192 | tf_op jit(solution)/shard_map/psum | solution.py:417
  263.2 0.1 fusion.28
  263.4 0.2 fusion.27
  263.6 0.4 fusion.21
  263.9 0.6 subtract_reduce_fusion
  264.6 0.4 subtract_convert_fusion
  265.0 0.1 divide_convert_fusion
  265.1 38.6 %psum.15 = f32[]{:T(128)} all-reduce(f32[]{:T(128)} %get-tuple-element.23), channel_id=1, replica_groups=mesh['dp'=8,'row'=4] {'dp','row'}, use_global_device_ids=true, to_apply=%region_15.16 | all-reduce | flops 1 | bytes 8 | tf_op jit(solution)/shard_map/psum | solution.py:430
  303.7 0.7 fusion.22.w_ref
  304.4 29.0 %exchange_weights.1 = (bf16[4,64,2176]{2,1,0:T(8,128)(2,1)}, bf16[4,8,64,256]{3,2,1,0:T(8,128)(2,1)}) custom-call(bf16[64,2176]{1,0:T(8,128)(2,1)} %fusion.22.w_ref), custom_call_target="tpu_custom_call" | custom-call | tf_op jit(solution)/shard_map/exchange_weights/pallas_call | solution.py:366
  333.4 1.3 slice_convert_fusion.3
  334.7 0.1 copy.53
  334.8 0.1 copy.55
  334.9 0.1 copy.54
  335.0 0.1 copy.56
  335.8 4.7 %fusion.10 = bf16[256,1024]{1,0:T(8,128)(2,1)} fusion(bf16[4,8,64,256]{3,2,1,0:T(8,128)(2,1)} %get-tuple-element.11, bf16[8,4,64,1024]{3,2,1,0:T(8,128)(2,1)} %bitcast.71), kind=kOutput, calls=%fused_computation.23 | convolution fusion | flops 1074003968 | bytes 5767168 | tf_op jit(solution)/shard_map/dot_general | solution.py:440
  340.5 2.3 fusion.9
  (18 shorter events, 0.1 us)
Async XLA Ops:
  0.6 231.7 %copy-start = (s32[16]{0:T(128)S(1)}, s32[16]{0:T(128)}, u32[]{:S(2)}) copy-start(s32[16]{0:T(128)} %param.13) | copy-start | bytes 196
  37.4 4.8 %copy-start.5 = (s32[256]{0:T(256)S(1)}, s32[256]{0:T(256)}, u32[]{:S(2)}) copy-start(s32[256]{0:T(256)} %param.12) | copy-start | bytes 3076
  37.4 196.2 %all-to-all-start.1 = ((bf16[8,256,1024]{2,1,0:T(8,128)(2,1)}), bf16[8,256,1024]{2,1,0:T(8,128)(2,1)}, u32[]{:S(2)}, u32[]{:S(2)}) async-start(bf16[8,256,1024]{2,1,0:T(8,128)(2,1)} %bitcast.54), calls=%async_computation.1 | async-start | bytes 8388608 | tf_op jit(solution)/shard_map/all_to_all | solution.py:34
  242.3 8.7 %copy-start.2 = (bf16[256,1024]{1,0:T(8,128)(2,1)S(1)}, bf16[256,1024]{1,0:T(8,128)(2,1)}, u32[]{:S(2)}) copy-start(bf16[256,1024]{1,0:T(8,128)(2,1)} %q_ref.1) | copy-start | bytes 1572868
  246.6 16.9 %copy-start.1 = (f32[64,2048]{1,0:T(8,128)S(1)}, f32[64,2048]{1,0:T(8,128)}, u32[]{:S(2)}) copy-start(f32[64,2048]{1,0:T(8,128)} %get-tuple-element.8) | copy-start | bytes 1572868
  334.9 5.7 %copy-start.3 = (bf16[4,64,2176]{2,1,0:T(8,128)(2,1)S(1)}, bf16[4,64,2176]{2,1,0:T(8,128)(2,1)}, u32[]{:S(2)}) copy-start(bf16[4,64,2176]{2,1,0:T(8,128)(2,1)} %get-tuple-element.9) | copy-start | bytes 3342340
  335.8 4.7 %copy-start.4 = (bf16[8,256,1024]{2,1,0:T(8,128)(2,1)S(1)}, bf16[8,256,1024]{2,1,0:T(8,128)(2,1)}, u32[]{:S(2)}) copy-start(bf16[8,256,1024]{2,1,0:T(8,128)(2,1)} %get-tuple-element.10) | copy-start | bytes 12582916

commit v2 on v1

--- a/solution.py
+++ b/solution.py
@@ -33,11 +33,9 @@
     picked = picked.reshape(asked_rows.shape[0], asked_rows.shape[1], width_dev)
     replies = lax.all_to_all(picked, "dp", split_axis=0, concat_axis=0, tiled=True)
     reply_rows = replies.reshape(n_data * capacity, width_dev)
-    hard_rows = [
-        jnp.take(reply_rows, target.reshape(row_count, hard_count)[:, h], axis=0, mode="clip")
-        for h in range(hard_count)
-    ]
-    return hard_rows
+    by_slot = target.reshape(row_count, hard_count).T.reshape(-1)
+    hard_rows = jnp.take(reply_rows, by_slot, axis=0, mode="clip")
+    return hard_rows.reshape(hard_count, row_count, width_dev)
 
 
 def gather_kernel(n, n_row, q_ref, p_ref, pall, qall, lsum, lpart, lrecv,
@@ -285,99 +283,172 @@
     )(queries, passages)
 
 
-def weights_kernel(n, n_row, columns, w_ref, wrow, wcol, dsend, drecv, rsend, rrecv, csend, crecv,
-                   own_sem):
+def weights_kernel(n, n_row, columns, w_ref, loss_ref, wrow, wcol, table, dsend, drecv, tsend,
+                   trecv, rsend, rrecv, own_sem):
     me = lax.axis_index("dp")
     r = lax.axis_index("row")
+    n_line = n_row // 2
+    y = r // 2
+    core = r % 2
+    partner = y * 2 + 1 - core
     barrier = pltpu.get_barrier_semaphore()
     for j in range(1, n):
         pl.semaphore_signal(
             barrier, inc=1, device_id=(lax.rem(me + j, n), r), device_id_type=MESH
         )
-    for k in range(1, n_row):
+    for k in range(1, n_line):
         pl.semaphore_signal(
-            barrier, inc=1, device_id=(me, lax.rem(r + k, n_row)), device_id_type=MESH
-        )
-    pl.semaphore_wait(barrier, n + n_row - 2)
+            barrier, inc=1, device_id=(me, lax.rem(r + 2 * k, n_row)), device_id_type=MESH
+        )
+    pl.semaphore_signal(barrier, inc=1, device_id=(me, partner), device_id_type=MESH)
+    pl.semaphore_wait(barrier, n + n_line - 1)
 
     def across(j):
         to = lax.rem(me + j, n)
         return pltpu.make_async_remote_copy(
             src_ref=w_ref.at[:, pl.ds(pl.multiple_of(to * columns, columns), columns)],
-            dst_ref=wcol.at[r, me],
+            dst_ref=wcol.at[y, core, me],
             send_sem=dsend.at[j - 1],
             recv_sem=drecv.at[j - 1],
             device_id=(to, r),
             device_id_type=MESH,
         )
 
-    def along(k):
-        return pltpu.make_async_remote_copy(
-            src_ref=w_ref,
-            dst_ref=wrow.at[r],
-            send_sem=rsend.at[k - 1],
-            recv_sem=rrecv.at[k - 1],
-            device_id=(me, lax.rem(r + k, n_row)),
-            device_id_type=MESH,
-        )
-
-    def spread(k):
-        return pltpu.make_async_remote_copy(
-            src_ref=wcol.at[r],
-            dst_ref=wcol.at[r],
-            send_sem=csend.at[k - 1],
-            recv_sem=crecv.at[k - 1],
-            device_id=(me, lax.rem(r + k, n_row)),
+    def tell(j):
+        return pltpu.make_async_remote_copy(
+            src_ref=loss_ref,
+            dst_ref=table.at[y, core, me],
+            send_sem=tsend.at[j - 1],
+            recv_sem=trecv.at[j - 1],
+            device_id=(lax.rem(me + j, n), r),
+            device_id_type=MESH,
+        )
+
+    def along(which, k):
+        out = (wrow, wcol, table)[which]
+        return pltpu.make_async_remote_copy(
+            src_ref=w_ref if which == 0 else out.at[y, core],
+            dst_ref=out.at[y, core],
+            send_sem=rsend.at[which, k - 1],
+            recv_sem=rrecv.at[which, k - 1],
+            device_id=(me, lax.rem(r + 2 * k, n_row)),
+            device_id_type=MESH,
+        )
+
+    def beside(which):
+        out = (wrow, wcol, table)[which]
+        return pltpu.make_async_remote_copy(
+            src_ref=out.at[:, core],
+            dst_ref=out.at[:, core],
+            send_sem=rsend.at[which, n_line - 1],
+            recv_sem=rrecv.at[which, n_line - 1],
+            device_id=(me, partner),
             device_id_type=MESH,
         )
 
     for j in range(1, n):
         across(j).start()
-    for k in range(1, n_row):
-        along(k).start()
-    own_row = pltpu.make_async_copy(w_ref, wrow.at[r], own_sem.at[0])
-    own_col = pltpu.make_async_copy(
-        w_ref.at[:, pl.ds(pl.multiple_of(me * columns, columns), columns)],
-        wcol.at[r, me],
-        own_sem.at[1],
-    )
-    own_row.start()
-    own_col.start()
-    own_col.wait()
+        tell(j).start()
+    for k in range(1, n_line):
+        along(0, k).start()
+    owns = (
+        pltpu.make_async_copy(w_ref, wrow.at[y, core], own_sem.at[0]),
+        pltpu.make_async_copy(
+            w_ref.at[:, pl.ds(pl.multiple_of(me * columns, columns), columns)],
+            wcol.at[y, core, me],
+            own_sem.at[1],
+        ),
+        pltpu.make_async_copy(loss_ref, table.at[y, core, me], own_sem.at[2]),
+    )
+    for own in owns:
+        own.start()
+    for own in owns:
+        own.wait()
     for j in range(1, n):
         across(j).wait_recv()
-    for k in range(1, n_row):
-        spread(k).start()
-    own_row.wait()
-    for k in range(1, n_row):
-        along(k).wait_recv()
-        spread(k).wait_recv()
+        tell(j).wait_recv()
+    for k in range(1, n_line):
+        along(1, k).start()
+        along(2, k).start()
+    for which in range(3):
+        for k in range(1, n_line):
+            along(which, k).wait_recv()
+        beside(which).start()
+    for which in range(3):
+        beside(which).wait_recv()
     for j in range(1, n):
         across(j).wait_send()
-    for k in range(1, n_row):
-        along(k).wait_send()
-        spread(k).wait_send()
-
-
-def exchange_weights(weights_ext, n, n_row, columns):
+        tell(j).wait_send()
+    for which in range(3):
+        for k in range(1, n_line):
+            along(which, k).wait_send()
+        beside(which).wait_send()
+
+
+def exchange_weights(weights_ext, loss_tile, n, n_row, columns):
     part, wide = weights_ext.shape
     vmem = pl.BlockSpec(memory_space=pltpu.VMEM)
     dma = pltpu.SemaphoreType.DMA
+    n_line = n_row // 2
     return pl.pallas_call(
         functools.partial(weights_kernel, n, n_row, columns),
         name="exchange_weights",
         out_shape=(
-            jax.ShapeDtypeStruct((n_row, part, wide), weights_ext.dtype),
-            jax.ShapeDtypeStruct((n_row, n, part, columns), weights_ext.dtype),
+            jax.ShapeDtypeStruct((n_line, 2, part, wide), weights_ext.dtype),
+            jax.ShapeDtypeStruct((n_line, 2, n, part, columns), weights_ext.dtype),
+            jax.ShapeDtypeStruct((n_line, 2, n) + loss_tile.shape, loss_tile.dtype),
         ),
-        in_specs=[vmem],
-        out_specs=(vmem, vmem),
+        in_specs=[vmem, vmem],
+        out_specs=(vmem, vmem, vmem),
         scratch_shapes=[
-            dma((n - 1,)), dma((n - 1,)), dma((n_row - 1,)), dma((n_row - 1,)),
-            dma((n_row - 1,)), dma((n_row - 1,)), dma((2,)),
+            dma((n - 1,)), dma((n - 1,)), dma((n - 1,)), dma((n - 1,)),
+            dma((3, n_line)), dma((3, n_line)), dma((3,)),
         ],
         compiler_params=pltpu.CompilerParams(collective_id=1, has_side_effects=True),
-    )(weights_ext)
+    )(weights_ext, loss_tile)
+
+
+def hard_kernel(n_row, x_ref, out, send, recv, own_sem):
+    me = lax.axis_index("dp")
+    r = lax.axis_index("row")
+    barrier = pltpu.get_barrier_semaphore()
+    for k in range(1, n_row):
+        pl.semaphore_signal(
+            barrier, inc=1, device_id=(me, lax.rem(r + k, n_row)), device_id_type=MESH
+        )
+    pl.semaphore_wait(barrier, n_row - 1)
+
+    def along(k):
+        return pltpu.make_async_remote_copy(
+            src_ref=x_ref,
+            dst_ref=out.at[r],
+            send_sem=send.at[k - 1],
+            recv_sem=recv.at[k - 1],
+            device_id=(me, lax.rem(r + k, n_row)),
+            device_id_type=MESH,
+        )
+
+    for k in range(1, n_row):
+        along(k).start()
+    own = pltpu.make_async_copy(x_ref, out.at[r], own_sem)
+    own.start()
+    own.wait()
+    for k in range(1, n_row):
+        along(k).wait()
+
+
+def gather_hard(partial_hard, n_row):
+    vmem = pl.BlockSpec(memory_space=pltpu.VMEM)
+    dma = pltpu.SemaphoreType.DMA
+    return pl.pallas_call(
+        functools.partial(hard_kernel, n_row),
+        name="gather_hard",
+        out_shape=jax.ShapeDtypeStruct((n_row,) + partial_hard.shape, partial_hard.dtype),
+        in_specs=[vmem],
+        out_specs=vmem,
+        scratch_shapes=[dma((n_row - 1,)), dma((n_row - 1,)), dma(())],
+        compiler_params=pltpu.CompilerParams(collective_id=2, has_side_effects=True),
+    )(partial_hard)
 
 
 def softmax_rows(summed, summed_hard, sources, block_source, first_row, logit_scale):
@@ -408,16 +479,16 @@
     part = row_count // n_row
     logit_scale = 1.0 / math.sqrt(D)
     hard_rows = fetch_hard(cached, hard_shard, hard_row, n_data)
-    hard_count = len(hard_rows)
+    hard_count = hard_rows.shape[0]
     pall, qall, summed = gather_and_logits(queries, passages, n_data, n_row)
-    q32 = queries.astype(jnp.float32)
-    partial_hard = jnp.stack(
-        [jnp.sum(q32 * rows.astype(jnp.float32), axis=1) for rows in hard_rows], axis=1
-    )
-    summed_hard = lax.psum(partial_hard, "row")
+    partial_hard = jnp.sum(
+        queries.astype(jnp.float32)[None] * hard_rows.astype(jnp.float32), axis=2
+    )
+    partial_hard = jnp.pad(partial_hard, ((0, -hard_count % 8), (0, 0)))
+    summed_hard = jnp.sum(gather_hard(partial_hard, n_row), axis=0)[:hard_count]
     row_at = lax.axis_index("row") * part
     first_row = lax.axis_index("dp") * row_count + row_at
-    my_hard = lax.dynamic_slice_in_dim(summed_hard, row_at, part, 0)
+    my_hard = lax.dynamic_slice_in_dim(summed_hard, row_at, part, 1).T
     my_source = lax.dynamic_slice_in_dim(query_source, row_at, part, 0)
     weights, hard_weights, local_loss = softmax_rows(
         summed, my_hard, my_source, block_source, first_row, logit_scale
@@ -426,8 +497,9 @@
     ext = jnp.concatenate(
         [weights, jnp.pad(hard_weights, ((0, 0), (0, LANES - hard_count)))], axis=1
     )
-    wrow, wcol = exchange_weights(ext, n_data, n_row, columns)
-    loss_sum = lax.psum(local_loss, ("dp", "row"))
+    loss_tile = jnp.full((8, LANES), local_loss, jnp.float32)
+    wrow, wcol, losses = exchange_weights(ext, loss_tile, n_data, n_row, columns)
+    loss_sum = jnp.sum(losses[:, :, :, 0, 0])
     mean_loss = loss_sum / (row_count * n_data)
     wrow = wrow.reshape(row_count, n_all + LANES)
     query_grad = jnp.dot(

time: 346 us -> 289 us (0.84)
  blocking collectives: 63.7 us -> 13.6 us
  local copies, waits for them, and re-layouts: 38.8 us -> 30.9 us
  Pallas kernels: 219 us -> 214 us
  other arithmetic: 8.38 us -> 13 us
    psum x2 -> x0, blocking collectives: 50.1 us -> none  [the longest x1 38.6 us: on_device(): loss_sum = lax.psum(local_loss, ('dp', 'row'))]
    gather x4 -> x1, local copies, waits for them, and re-layouts: 17.3 us -> 7.76 us  [fetch_hard(): hard_rows = jnp.take(reply_rows, by_slot, axis=0, mode='clip')]
    pallas_call x1, Pallas kernels: 29 us -> 20.7 us  [exchange_weights(): pl.pallas_call(functools.partial(weights_kernel, n, n_row, columns), name...]
    pallas_call x0 -> x1, Pallas kernels: none -> 5.01 us  [gather_hard(): pl.pallas_call(functools.partial(hard_kernel, n_row), name='gather_hard',...]
    reduce_sum x1 -> x4, other arithmetic: 0.6 us -> 4.47 us  [the longest x1 1.79 us: on_device(): jnp.sum(queries.astype(jnp.float32)[None] * hard_rows.astype(jnp.float32)...]
  transfers between devices with their start and end apart: 1 -> 1, of which waited for: 0 -> 0; matrix products, arithmetic and copies ran while one was open for 1% -> 1% of each run, Pallas kernels for 55% -> 65%
where the time goes in v2:
time: 289 us; the launch traced here: 288 us
  Pallas kernels  214 us (74%)
  local copies, waits for them, and re-layouts  30.9 us (11%)
  blocking collectives  13.6 us (5%)
  other arithmetic  13 us (4%)
  matrix products  9.2 us (3%)
  starting transfers between devices  4.73 us (2%)
    pallas_call x1, Pallas kernels, gather_and_logits(): pl.pallas_call(functools.partial(gather_kernel, n, n_row), name='gather_l...  189 us
    pallas_call x1, Pallas kernels, exchange_weights(): pl.pallas_call(functools.partial(weights_kernel, n, n_row, columns), name...  20.7 us
    gather x1, local copies, waits for them, and re-layouts, fetch_hard(): picked = jnp.take(cached, asked_rows.reshape(-1), axis=0, mode='clip')  13.7 us
    all_to_all x1, blocking collectives, fetch_hard(): lax.all_to_all(requests, 'dp', split_axis=0, concat_axis=0, tiled=True)  13.6 us
    gather x1, local copies, waits for them, and re-layouts, fetch_hard(): hard_rows = jnp.take(reply_rows, by_slot, axis=0, mode='clip')  7.76 us
  transfers between devices with their start and end apart: 1, of which 0 were waited for; matrix products, arithmetic and copies ran while one was open for 1% of the time, Pallas kernels for 65%

profile of v2, /device:TPU:0, one launch (start us, length us, event | category | flops | bytes accessed | tf_op | source)
XLA Modules:
  0.0 288.3 jit_solution(2632461046657408227)
XLA Ops:
  0.6 0.0 copy-start
  0.6 0.8 copy.30
  1.5 0.1 eq.45
  1.6 0.1 eq.41
  1.7 2.3 reduce-window.6
  4.0 0.3 slice_reduce_fusion
  4.3 0.2 reduce-window.9
  4.4 0.1 add_bitcast_fusion.1
  4.6 0.1 reduce_sum.78
  4.7 0.1 mul.110
  4.8 0.8 copy.33
  5.7 0.1 reshape.155
  5.8 4.3 %scatter_custom_fusion = s32[2048]{0:T(1024)S(1)} fusion(s32[1024]{0:T(1024)S(1)} %bitcast.69, s32[1024]{0:T(1024)S(1)} %reshape.155, s32[]{:T(128)} %constant.15.clone.1), kind=kCustom, calls=%fused_computation.49 | custom fusion | bytes 8196 | tf_op jit(solution)/shard_map/scatter | solution.py:29
  10.1 13.6 %all_to_all.14 = s32[8,1,256]{2,1,0:T(1,128)S(1)} all-to-all(s32[8,1,256]{2,1,0:T(1,128)S(1)} %bitcast.64), channel_id=1, replica_groups=mesh['dp'=8,'row'=4] {'dp'}, dimensions={0} | all-to-all | bytes 16384 | tf_op jit(solution)/shard_map/all_to_all | solution.py:31
  23.7 13.7 %gather_fusion = bf16[2048,1024]{1,0:T(8,128)(2,1)} fusion(bf16[2048,1024]{1,0:T(8,128)(2,1)} %param.9, s32[2048]{0:T(1024)S(1)} %broadcast_clamp_fusion), kind=kCustom, calls=%fused_computation | custom fusion | bytes 8396800 | tf_op jit(solution)/shard_map/jit(_take)/gather | solution.py:32
  37.4 4.7 %all-to-all-start.1 = ((bf16[8,256,1024]{2,1,0:T(8,128)(2,1)}), bf16[8,256,1024]{2,1,0:T(8,128)(2,1)}, u32[]{:S(2)}, u32[]{:S(2)}) async-start(bf16[8,256,1024]{2,1,0:T(8,128)(2,1)} %bitcast.59), calls=%async_computation.1 | async-start | bytes 8388608 | tf_op jit(solution)/shard_map/all_to_all | solution.py:34
  42.2 0.1 copy.34
  42.3 1.1 convert_element_type.53
  43.4 188.5 %gather_logits.1 = (bf16[8,256,1024]{2,1,0:T(8,128)(2,1)}, bf16[8,256,1024]{2,1,0:T(8,128)(2,1)}, f32[64,2048]{1,0:T(8,128)}) custom-call(bf16[256,1024]{1,0:T(8,128)(2,1)} %q_ref.1, bf16[256,1024]{1,0:T(8,128)(2,1)} %p_ref.1), custom_call_target="tpu_custom_call" | custom-call | tf_op jit(solution)/shard_map/gather_logits/pallas_call | solution.py:261
  231.9 0.1 dynamic_slice.6
  232.0 0.1 broadcast_bitcast_fusion
  232.1 1.3 fusion.28
  233.4 0.0 all-to-all-done.1
  233.4 7.8 %gather_fusion.1 = bf16[1024,1024]{1,0:T(8,128)(2,1)S(1)} fusion(bf16[2048,1024]{1,0:T(8,128)(2,1)} %bitcast.7, s32[1024]{0:T(1024)S(1)} %broadcast_clamp_fusion.1), kind=kCustom, calls=%fused_computation.1 | custom fusion | bytes 4198400 | tf_op jit(solution)/shard_map/jit(_take)/gather | solution.py:37
  241.2 1.8 fusion
  243.0 0.6 pad.8.x_ref
  243.6 5.0 %gather_hard.1 = f32[4,8,256]{2,1,0:T(8,128)} custom-call(f32[8,256]{1,0:T(8,128)} %pad.8.x_ref), custom_call_target="tpu_custom_call" | custom-call | tf_op jit(solution)/shard_map/gather_hard/pallas_call | solution.py:443
  248.6 0.8 reduce_sum.80
  249.4 0.1 constant_dynamic-slice_fusion
  249.4 0.1 copy.42
  249.5 0.1 multiply_reduce_fusion
  249.7 0.2 fusion.24
  249.9 0.4 select_reduce_fusion
  250.2 0.6 subtract_reduce_fusion
  250.9 0.4 subtract_convert_fusion
  251.3 0.1 fusion.25
  251.4 0.7 fusion.19.w_ref
  252.1 1.2 broadcast_in_dim.40.loss_ref
  253.3 20.7 %exchange_weights.1 = (bf16[2,2,64,2176]{3,2,1,0:T(8,128)(2,1)}, bf16[2,2,8,64,256]{4,3,2,1,0:T(8,128)(2,1)}, f32[2,2,8,8,128]{4,3,2,1,0:T(8,128)}) custom-call(bf16[64,2176]{1,0:T(8,128)(2,1)} %fusion.19.w_ref, f32[8,128]{1,0:T(8,128)} %broadcast_in_dim.40.loss_ref), custom_call_target="tpu_custom_call" | custom-call | tf_op jit(solution)/shard_map/exchange_weights/pallas_call | solution.py:393
  274.1 1.5 slice_reduce_fusion.1
  275.6 1.3 slice_convert_fusion.3
  277.0 0.1 copy.49
  277.1 0.1 copy.51
  277.1 0.1 copy.50
  277.2 0.1 copy.52
  277.3 4.7 %fusion.11 = bf16[256,1024]{1,0:T(8,128)(2,1)} fusion(bf16[4,8,64,256]{3,2,1,0:T(8,128)(2,1)} %bitcast.76, bf16[8,4,64,1024]{3,2,1,0:T(8,128)(2,1)} %bitcast.75), kind=kOutput, calls=%fused_computation.14 | convolution fusion | flops 1074003968 | bytes 5767168 | tf_op jit(solution)/shard_map/dot_general | solution.py:512
  282.6 0.0 copy-done.3
  282.7 4.5 %fusion.10 = bf16[256,1024]{1,0:T(8,128)(2,1)} fusion(bf16[2048,1024]{1,0:T(8,128)(2,1)} %bitcast.74, bf16[256,2176]{1,0:T(8,128)(2,1)S(1)} %bitcast.62, bf16[1024,1024]{1,0:T(8,128)(2,1)S(1)} %gather_fusion.1, f32[256]{0:T(256)S(1)} %bitcast.73, f32[256]{0:T(256)S(1)} %bitcast.71, f32[256]{0:T(256)S(1)} %bitcast.72, f32[256]{0:T(256)S(1)} %bitcast.70), kind=kOutput, calls=%fused_computation.13 | convolution fusion | flops 1077149696 | bytes 7868416 | tf_op jit(solution)/shard_map/dot_general | solution.py:505
  (18 shorter events, 0.1 us)
Async XLA Ops:
  0.6 231.4 %copy-start = (s32[16]{0:T(128)S(1)}, s32[16]{0:T(128)}, u32[]{:S(2)}) copy-start(s32[16]{0:T(128)} %param.13) | copy-start | bytes 196
  37.4 4.8 %copy-start.2 = (bf16[256,1024]{1,0:T(8,128)(2,1)S(1)}, bf16[256,1024]{1,0:T(8,128)(2,1)}, u32[]{:S(2)}) copy-start(bf16[256,1024]{1,0:T(8,128)(2,1)} %q_ref.1) | copy-start | bytes 1572868
  37.4 194.5 %copy-start.4 = (s32[256]{0:T(256)S(1)}, s32[256]{0:T(256)}, u32[]{:S(2)}) copy-start(s32[256]{0:T(256)} %param.12) | copy-start | bytes 3076
  37.4 196.0 %all-to-all-start.1 = ((bf16[8,256,1024]{2,1,0:T(8,128)(2,1)}), bf16[8,256,1024]{2,1,0:T(8,128)(2,1)}, u32[]{:S(2)}, u32[]{:S(2)}) async-start(bf16[8,256,1024]{2,1,0:T(8,128)(2,1)} %bitcast.59), calls=%async_computation.1 | async-start | bytes 8388608 | tf_op jit(solution)/shard_map/all_to_all | solution.py:34
  233.4 16.5 %copy-start.1 = (f32[64,2048]{1,0:T(8,128)S(1)}, f32[64,2048]{1,0:T(8,128)}, u32[]{:S(2)}) copy-start(f32[64,2048]{1,0:T(8,128)} %get-tuple-element.9) | copy-start | bytes 1572868
  277.1 5.5 %copy-start.3 = (bf16[2,2,64,2176]{3,2,1,0:T(8,128)(2,1)S(1)}, bf16[2,2,64,2176]{3,2,1,0:T(8,128)(2,1)}, u32[]{:S(2)}) copy-start(bf16[2,2,64,2176]{3,2,1,0:T(8,128)(2,1)} %get-tuple-element.11) | copy-start | bytes 3342340
